TPU v7x, 32 devices: a whole 2x2x4 slice. The times are simulated.
32 devices in a mesh: dp: 2 (over x), ctx: 8 (over z, y), head: 2 (over core).
Axes of the slice: x: 2, y: 2, z: 4, core: 2. Of those that a mesh axis runs over, the one named last changes fastest.
Arguments:
- queries: bfloat16 [2, 1024, 4096], P('dp', 'ctx', 'head'), may hold values from -200 to 200
- targets: bfloat16 [2, 1024, 4096], P('dp', 'ctx', 'head'), may hold values from -3 to 3
- document_keys: bfloat16 [2, 1024, 256], P('dp', 'ctx', 'head'), may hold values from -6 to 6
- document_values: bfloat16 [2, 1024, 256], P('dp', 'ctx', 'head'), may hold values from -6 to 6
- doc_pos: int32 [2, 1024], P('dp', 'ctx'), may hold values from 0 to 1023, each once within a row
- cart_keys: bfloat16 [128, 256], P('ctx', 'head'), may hold values from -8 to 8
- cartridge_values: bfloat16 [128, 256], P('ctx', 'head'), may hold values from -6 to 6
- master: float32 [128, 2, 256], P('ctx', 'head', 'dp'), may hold values from -5 to 5
- first_moment1: float32 [128, 2, 256], P('ctx', 'head', 'dp'), may hold values from -4 to 4
- second_moment2: float32 [128, 2, 256], P('ctx', 'head', 'dp'), may hold values from 0.1 to 2
Outputs:
- new_out: bfloat16 [2, 1024, 4096], P('dp', 'ctx', 'head')
- new_master: float32 [128, 2, 256], P('ctx', 'head', 'dp')
- new_moment1: float32 [128, 2, 256], P('ctx', 'head', 'dp')
- new_moment2: float32 [128, 2, 256], P('ctx', 'head', 'dp')
Inputs may be any that keep to these rules, and one draw needn't show every extreme that they name: Each row of doc_pos holds every position of the document once.
All inputs are finite; a program needn't handle non-finite values.
Results may differ from a plain program's by a relative error of at most 0.015.
Values may be sent and summed in bfloat16 or wider, within the bound.
No kernel may reach another device: no remote copies, remote signals or barrier semaphores. Data moves between devices by JAX's collectives and lax.ppermute only.
A program may use at most 64 MiB of HBM per device.

v0:
```python
import math
import jax
import jax.numpy as jnp
from jax import lax
from jax.sharding import PartitionSpec as P

beta_one = 0.8
beta_two = 0.95
learn_rate = 0.1
adam_eps = 1e-08
norm_eps = 1e-06
neg_big = -1e30


def scores_of(left, right):
    return lax.dot_general(
        left, right, (((1,), (1,)), ((), ())), preferred_element_type=jnp.float32
    )


def online(state, scores, values, allowed):
    old_top, old_total, old_acc = state
    if allowed is not None:
        scores = jnp.where(allowed, scores, neg_big)
    new_top = jnp.maximum(old_top, jnp.max(scores, axis=1))
    weights = jnp.exp(scores - new_top[:, None])
    if allowed is not None:
        weights = jnp.where(allowed, weights, 0.0)
    factor = jnp.exp(old_top - new_top)
    total = old_total * factor + jnp.sum(weights, axis=1)
    accum = old_acc * factor[:, None] + jnp.dot(
        weights.astype(jnp.bfloat16), values, preferred_element_type=jnp.float32
    )
    return (new_top, total, accum)


def combine(first, second):
    top = jnp.maximum(first[0], second[0])
    f_one = jnp.exp(first[0] - top)
    f_two = jnp.exp(second[0] - top)
    total = first[1] * f_one + second[1] * f_two
    accum = first[2] * f_one[:, None] + second[2] * f_two[:, None]
    return (top, total, accum)


def local(
    queries,
    targets,
    document_keys,
    document_values,
    doc_pos,
    cart_keys,
    cartridge_values,
    master,
    first_moment1,
    second_moment2,
):
    head_dim = document_keys.shape[2]
    rows = queries.shape[1]
    group = queries.shape[2] // head_dim
    scale = head_dim ** (-0.5)
    flat_query = queries[0].reshape(rows * group, head_dim)
    query_pos = jnp.repeat(doc_pos[0], group)
    all_pos = lax.all_gather(doc_pos[0], "ctx", axis=0, tiled=True)
    cart_k_all, cart_v_all = (
        lax.all_gather(cart_keys, "ctx", axis=0, tiled=True),
        lax.all_gather(cartridge_values, "ctx", axis=0, tiled=True),
    )
    empty = (
        jnp.full((rows * group,), neg_big, jnp.float32),
        jnp.zeros((rows * group,), jnp.float32),
        jnp.zeros((rows * group, head_dim), jnp.float32),
    )

    def cart_part(keys_all, values_all):
        return online(empty, scores_of(flat_query, keys_all) * scale, values_all, None)

    state = empty
    keys = lax.all_gather(document_keys, "ctx", axis=1, tiled=True)[0]
    values = lax.all_gather(document_values, "ctx", axis=1, tiled=True)[0]
    count = keys.shape[0]
    step_rows = math.gcd(count, 512)

    def inner(carry, index):
        first = index * step_rows
        key_block = lax.dynamic_slice_in_dim(keys, first, step_rows)
        value_block = lax.dynamic_slice_in_dim(values, first, step_rows)
        pos_block = lax.dynamic_slice_in_dim(all_pos, first, step_rows)
        allowed = pos_block[None, :] <= query_pos[:, None]
        scores = scores_of(flat_query, key_block) * scale
        return (online(carry, scores, value_block, allowed), None)

    state, _ = lax.scan(inner, state, jnp.arange(count // step_rows, dtype=jnp.int32))
    merged = combine(cart_part(cart_k_all, cart_v_all), state)
    top, total = (merged[0], merged[1])
    out = merged[2] / total[:, None]
    d_out = out - targets[0].reshape(rows * group, head_dim).astype(jnp.float32)
    delta = jnp.sum(d_out * out, axis=1)
    d_out_b = d_out.astype(jnp.bfloat16)
    width = master.shape[2]
    count_all = master.size * lax.axis_size("dp") * lax.axis_size("ctx") * lax.axis_size("head")
    probs = jnp.exp(scores_of(flat_query, cart_k_all) * scale - top[:, None]) / total[:, None]
    d_probs = scores_of(d_out_b, cart_v_all)
    d_scores = probs * (d_probs - delta[:, None])
    grad_k = (
        lax.dot_general(
            d_scores.astype(jnp.bfloat16),
            flat_query,
            (((0,), (0,)), ((), ())),
            preferred_element_type=jnp.float32,
        )
        * scale
    )
    grad_v = lax.dot_general(
        probs.astype(jnp.bfloat16),
        d_out_b,
        (((0,), (0,)), ((), ())),
        preferred_element_type=jnp.float32,
    )
    term = lax.psum_scatter(
        jnp.concatenate([grad_k, grad_v], axis=1).astype(jnp.bfloat16),
        "ctx",
        scatter_dimension=0,
        tiled=True,
    ).astype(jnp.float32)
    full = lax.psum(term, "dp")
    squares = lax.psum(jnp.sum(full * full), ("ctx", "head"))
    owned = lax.dynamic_slice_in_dim(full, lax.axis_index("dp") * width, width, 1)
    rms = jnp.sqrt(squares / count_all + norm_eps)
    normed = (owned / rms).reshape(master.shape)
    new_moment1 = beta_one * first_moment1 + (1.0 - beta_one) * normed
    new_moment2 = beta_two * second_moment2 + (1.0 - beta_two) * normed * normed
    new_master = master - learn_rate * new_moment1 / (jnp.sqrt(new_moment2) + adam_eps)
    copies = new_master.reshape(master.shape[0], width).astype(jnp.bfloat16)
    columns = lax.all_gather(copies, "dp", axis=1, tiled=True)
    fresh = lax.all_gather(columns, "ctx", axis=0, tiled=True)
    final = combine(cart_part(fresh[:, :head_dim], fresh[:, head_dim:]), state)
    new_out = (final[2] / final[1][:, None]).astype(jnp.bfloat16).reshape(1, rows, group * head_dim)
    return (new_out, new_master, new_moment1, new_moment2)


def solution(mesh):
    in_specs = (
        P("dp", "ctx", "head"),
        P("dp", "ctx", "head"),
        P("dp", "ctx", "head"),
        P("dp", "ctx", "head"),
        P("dp", "ctx"),
        P("ctx", "head"),
        P("ctx", "head"),
        P("ctx", "head", "dp"),
        P("ctx", "head", "dp"),
        P("ctx", "head", "dp"),
    )
    out_specs = (
        P("dp", "ctx", "head"),
        P("ctx", "head", "dp"),
        P("ctx", "head", "dp"),
        P("ctx", "head", "dp"),
    )
    return jax.shard_map(local, mesh=mesh, in_specs=in_specs, out_specs=out_specs, check_vma=False)
```

profile of v0, /device:TPU:0, one launch (start us, length us, event | category | flops | bytes accessed | tf_op | source)
XLA Modules:
  0.0 330.7 jit_solution(10116764384674142388)
XLA Ops:
  7.2 0.0 reduce-scatter.4.cloned.1.call-start
  7.2 22.5 %all-gather = s32[1,1024]{1,0:T(1,128)S(1)} all-gather(s32[1,128]{1,0:T(1,128)} %param.16), channel_id=2, replica_groups=mesh['dp'=2,'ctx'=8,'head'=2] {'ctx'}, dimensions={1}, use_global_device_ids=true | all-gather | bytes 4608 | tf_op jit(solution)/shard_map/all_gather | solution.py:64
  29.7 30.9 %all_gather.23 = bf16[1,1024,128]{2,1,0:T(8,128)(2,1)S(1)} all-gather(bf16[1,128,128]{2,1,0:T(8,128)(2,1)} %param.14), channel_id=1, replica_groups=mesh['dp'=2,'ctx'=8,'head'=2] {'ctx'}, dimensions={1}, use_global_device_ids=true | all-gather | bytes 294912 | tf_op jit(solution)/shard_map/all_gather | solution.py:79
  60.6 1.3 reshape_squeeze.4
  61.9 31.0 %all_gather.24 = bf16[1,1024,128]{2,1,0:T(8,128)(2,1)S(1)} all-gather(bf16[1,128,128]{2,1,0:T(8,128)(2,1)} %param.15), channel_id=1, replica_groups=mesh['dp'=2,'ctx'=8,'head'=2] {'ctx'}, dimensions={1}, use_global_device_ids=true | all-gather | bytes 294912 | tf_op jit(solution)/shard_map/all_gather | solution.py:80
  92.9 0.0 copy-start.1
  92.9 0.0 copy-start.5
  92.9 23.1 %while.15 = (s32[]{:T(128)}, f32[2048]{0:T(1024)S(1)}, f32[2048]{0:T(1024)S(1)}, f32[2048,128]{1,0:T(8,128)}, s32[2]{0:T(128)S(1)}, /*index=5*/s32[1024]{0:T(102...) while((s32[]{:T(128)}, f32[2048]{0:T(1024)S(1)}, ...), condition=%wide.region_4.5_spmd.clone, body=%wide.region_1.4_spmd.clone.sunk | while | flops 554444800 | bytes 32434936 | solution.py:93
  92.9 0.8 broadcast_in_dim.101
  93.7 0.1 le.61
  93.8 0.6 dynamic_slice.40
  95.0 0.1 dynamic_slice.41
  95.1 2.7 fusion.74
  97.8 0.0 copy-start
  97.8 3.5 %fusion.75 = f32[2048]{0:T(1024)S(1)} fusion(f32[512,2048]{1,0:T(8,128)} %get-tuple-element.222, f32[2048]{0:T(1024)S(1)} %select_maximum_fusion.2, s32[2048]{0:T(1024)S(1)} %le.61, s32[512]{0:T(512)S(1)} %dynamic_slice.41), kind=kLoop, calls=%fused_computation.6.clone.1 | loop fusion | flops 6289408 | bytes 4220928 | tf_op jit(solution)/shard_map/while/body/eval_jaxpr/reduce_sum | solution.py:30
  101.3 0.0 copy-done
  101.3 2.5 convolution_add_fusion.4
  103.9 0.7 broadcast_in_dim.101
  104.6 0.1 le.61
  104.7 0.6 dynamic_slice.40
  105.9 0.1 dynamic_slice.41
  106.0 2.7 fusion.74
  108.7 0.0 copy-start
  108.7 3.5 %fusion.75 = f32[2048]{0:T(1024)S(1)} fusion(f32[512,2048]{1,0:T(8,128)} %get-tuple-element.222, f32[2048]{0:T(1024)S(1)} %select_maximum_fusion.2, s32[2048]{0:T(1024)S(1)} %le.61, s32[512]{0:T(512)S(1)} %dynamic_slice.41), kind=kLoop, calls=%fused_computation.6.clone.1 | loop fusion | flops 6289408 | bytes 4220928 | tf_op jit(solution)/shard_map/while/body/eval_jaxpr/reduce_sum | solution.py:30
  112.2 0.0 copy-done
  112.2 3.8 %convolution_add_fusion.4 = f32[2048,128]{1,0:T(8,128)} fusion(f32[512,2048]{1,0:T(8,128)S(1)} %copy-done, f32[2048]{0:T(1024)S(1)} %select_maximum_fusion.2, s32[2048]{0:T(1024)S(1)} %le.61, s32[512]{0:T(512)S(1)} %dynamic_slice.41, f32[2048,128]{1,0:T(8,128)} %get-tuple-element.242, f32[2048]{0:T(1024)S(1)} %get-tuple-element.224, ...), kind=kOutput, calls=%fused_computation.4.clone.1 | convolution fusion | flops 275513344 | bytes 6449157 | tf_op jit(solution)/shard_map/while/body/eval_jaxpr/dot_general | solution.py:31
  116.0 0.0 copy-done.1
  116.0 0.0 copy-start.6
  116.0 0.2 reshape.48
  116.2 0.3 copy.47
  116.6 0.0 copy-done.5
  116.6 30.6 %all_gather.21 = bf16[128,128]{1,0:T(8,128)(2,1)S(1)} all-gather(bf16[16,128]{1,0:T(8,128)(2,1)S(1)} %copy-done.5), channel_id=1, replica_groups=mesh['dp'=2,'ctx'=8,'head'=2] {'ctx'}, dimensions={0}, use_global_device_ids=true | all-gather | bytes 36864 | tf_op jit(solution)/shard_map/all_gather | solution.py:66
  147.2 0.3 fusion.54
  147.5 2.6 copy.46
  150.0 0.0 copy-done.6
  150.0 30.6 %all_gather.25 = bf16[128,128]{1,0:T(8,128)(2,1)S(1)} all-gather(bf16[16,128]{1,0:T(8,128)(2,1)S(1)} %copy-done.6), channel_id=1, replica_groups=mesh['dp'=2,'ctx'=8,'head'=2] {'ctx'}, dimensions={0}, use_global_device_ids=true | all-gather | bytes 36864 | tf_op jit(solution)/shard_map/all_gather | solution.py:67
  180.6 0.2 fusion.34
  180.8 1.7 multiply_reduce_fusion
  182.6 0.0 copy-start.2
  182.6 0.0 copy-start.3
  182.6 0.0 copy-start.4
  182.6 0.4 convolution_convert_fusion
  183.0 0.6 fusion.32
  183.6 0.7 copy.56
  184.4 0.0 reduce-scatter.4.cloned.1.call-update
  184.4 59.8 %reduce-scatter.4.cloned.1.call-done = bf16[16,256]{1,0:T(8,128)(2,1)} async-done(((bf16[128,256]{1,0:T(8,128)(2,1)}), bf16[16,256]{1,0:T(8,128)(2,1)}) %reduce-scatter.4.cloned.1.call-update) | async-done | bytes 8208 | tf_op jit(solution)/shard_map/reduce_scatter | solution.py:120
  244.2 8.7 %psum.14 = f32[16,256]{1,0:T(8,128)S(1)} all-reduce(bf16[16,256]{1,0:T(8,128)(2,1)} %reduce-scatter.4.cloned.1.call-done), channel_id=1, replica_groups=mesh['dp'=2,'ctx'=8,'head'=2] {'dp'}, use_global_device_ids=true, to_apply=%region_8.9 | all-reduce | flops 4096 | bytes 24576 | tf_op jit(solution)/shard_map/psum | solution.py:126
  252.9 0.6 multiply_reduce_fusion.1
  253.5 30.1 %psum.15 = f32[]{:T(128)} all-reduce(f32[]{:T(128)} %multiply_reduce_fusion.1), channel_id=1, replica_groups=mesh['dp'=2,'ctx'=8,'head'=2] {'ctx','head'}, use_global_device_ids=true, to_apply=%region_10.11 | all-reduce | flops 1 | bytes 8 | tf_op jit(solution)/shard_map/psum | solution.py:127
  284.3 0.0 copy-done.2
  284.3 0.0 copy-done.3
  284.3 0.0 copy-done.4
  284.3 0.6 fusion.52
  285.0 4.3 %all-gather.1 = bf16[16,1,256]{2,0,1:T(8,128)(2,1)S(1)} all-gather(bf16[16,1,128]{2,0,1:T(8,128)(2,1)S(1)} %get-tuple-element.138), channel_id=3, replica_groups=mesh['dp'=2,'ctx'=8,'head'=2] {'dp'}, dimensions={2}, use_global_device_ids=true | all-gather | bytes 12288 | tf_op jit(solution)/shard_map/all_gather | solution.py:135
  289.3 30.5 %all-gather.2 = bf16[128,1,256]{2,0,1:T(8,128)(2,1)S(1)} all-gather(bf16[16,1,256]{2,0,1:T(8,128)(2,1)S(1)} %all-gather.1), channel_id=4, replica_groups=mesh['dp'=2,'ctx'=8,'head'=2] {'ctx'}, dimensions={0}, use_global_device_ids=true | all-gather | bytes 73728 | tf_op jit(solution)/shard_map/all_gather | solution.py:136
  319.8 0.3 fusion.55
  320.1 0.2 fusion.35
  320.3 2.5 fusion.28
  322.8 1.0 reshape.47
  (15 shorter events, 0.1 us)
Async XLA Ops:
  7.2 237.0 %reduce-scatter.4.cloned.1.call-start = ((), (), s32[]{:S(2)}) async-start(), calls=%async_computation.1 | async-start | bytes 73728 | tf_op jit(solution)/shard_map/reduce_scatter | solution.py:120
  92.9 23.1 %copy-start.1 = (bf16[1,128,2048]{2,1,0:T(8,128)(2,1)S(1)}, bf16[1,128,2048]{2,1,0:T(8,128)(2,1)}, u32[]{:S(2)}) copy-start(bf16[1,128,2048]{2,1,0:T(8,128)(2,1)} %param.13) | copy-start | bytes 1572868
  92.9 23.7 %copy-start.5 = (bf16[16,128]{1,0:T(8,128)(2,1)S(1)}, bf16[16,128]{1,0:T(8,128)(2,1)}, u32[]{:S(2)}) copy-start(bf16[16,128]{1,0:T(8,128)(2,1)} %param.17) | copy-start | bytes 12292
  97.8 3.6 %copy-start = (f32[512,2048]{1,0:T(8,128)S(1)}, f32[512,2048]{1,0:T(8,128)}, u32[]{:S(2)}) copy-start(f32[512,2048]{1,0:T(8,128)} %get-tuple-element.222) | copy-start | bytes 12582916 | tf_op jit(solution)/shard_map/while
  108.7 3.6 %copy-start = (f32[512,2048]{1,0:T(8,128)S(1)}, f32[512,2048]{1,0:T(8,128)}, u32[]{:S(2)}) copy-start(f32[512,2048]{1,0:T(8,128)} %get-tuple-element.222) | copy-start | bytes 12582916 | tf_op jit(solution)/shard_map/while
  116.0 34.0 %copy-start.6 = (bf16[16,128]{1,0:T(8,128)(2,1)S(1)}, bf16[16,128]{1,0:T(8,128)(2,1)}, u32[]{:S(2)}) copy-start(bf16[16,128]{1,0:T(8,128)(2,1)} %param.18) | copy-start | bytes 12292
  182.6 101.7 %copy-start.2 = (f32[16,1,128]{2,1,0:T(1,128)S(1)}, f32[16,1,128]{2,1,0:T(1,128)}, u32[]{:S(2)}) copy-start(f32[16,1,128]{2,1,0:T(1,128)} %param.19) | copy-start | bytes 24580
  182.6 101.7 %copy-start.3 = (f32[16,1,128]{2,1,0:T(1,128)S(1)}, f32[16,1,128]{2,1,0:T(1,128)}, u32[]{:S(2)}) copy-start(f32[16,1,128]{2,1,0:T(1,128)} %param.20) | copy-start | bytes 24580
  182.6 101.7 %copy-start.4 = (f32[16,1,128]{2,1,0:T(1,128)S(1)}, f32[16,1,128]{2,1,0:T(1,128)}, u32[]{:S(2)}) copy-start(f32[16,1,128]{2,1,0:T(1,128)} %param.21) | copy-start | bytes 24580
Sparse Core Ops, SparseCore 0:
  184.5 59.5 reduce-scatter.3
where the time goes:
time: 331 us
  blocking collectives  219 us (66%)
  waiting for transfers between devices  59.8 us (18%)
  matrix products  17.4 us (5%)
  between operations  14.9 us (5%)
  local copies, waits for them, and re-layouts  9.2 us (3%)
  other arithmetic  8.7 us (3%)
    reduce_scatter x1, waiting for transfers between devices, local(): lax.psum_scatter(jnp.concatenate([grad_k, grad_v], axis=1).astype(jnp.bfl...  59.8 us
    all_gather x1, blocking collectives, local(): values = lax.all_gather(document_values, 'ctx', axis=1, tiled=True)[0]  31 us
    all_gather x1, blocking collectives, local(): keys = lax.all_gather(document_keys, 'ctx', axis=1, tiled=True)[0]  30.9 us
    all_gather x1, blocking collectives, local(): lax.all_gather(cart_keys, 'ctx', axis=0, tiled=True)  30.6 us
    all_gather x1, blocking collectives, local(): lax.all_gather(cartridge_values, 'ctx', axis=0, tiled=True)  30.6 us
    all_gather x1, blocking collectives, local(): fresh = lax.all_gather(columns, 'ctx', axis=0, tiled=True)  30.5 us
    psum x1, blocking collectives, local(): squares = lax.psum(jnp.sum(full * full), ('ctx', 'head'))  30.1 us
    all_gather x1, blocking collectives, local(): all_pos = lax.all_gather(doc_pos[0], 'ctx', axis=0, tiled=True)  22.5 us
  transfers between devices with their start and end apart: 1, of which 1 were waited for; matrix products, arithmetic and copies ran while one was open for 0% of the time, Pallas kernels for 0%

commit v1 on v0

--- a/solution.py
+++ b/solution.py
@@ -133,7 +133,12 @@
     new_master = master - learn_rate * new_moment1 / (jnp.sqrt(new_moment2) + adam_eps)
     copies = new_master.reshape(master.shape[0], width).astype(jnp.bfloat16)
     columns = lax.all_gather(copies, "dp", axis=1, tiled=True)
-    fresh = lax.all_gather(columns, "ctx", axis=0, tiled=True)
+    ring = [columns]
+    for hop in range(7):
+        ring.append(lax.ppermute(ring[-1], "ctx", [(dev, (dev + 1) % 8) for dev in range(8)]))
+    fresh = jnp.roll(
+        jnp.concatenate(ring[::-1], axis=0), (lax.axis_index("ctx") + 1) * ring[0].shape[0], axis=0
+    )
     final = combine(cart_part(fresh[:, :head_dim], fresh[:, head_dim:]), state)
     new_out = (final[2] / final[1][:, None]).astype(jnp.bfloat16).reshape(1, rows, group * head_dim)
     return (new_out, new_master, new_moment1, new_moment2)

time: 331 us -> 345 us (1.042)
  waiting for transfers between devices: 59.8 us -> 104 us
  blocking collectives: 219 us -> 189 us
    ppermute x0 -> x7, waiting for transfers between devices: none -> 44.4 us  [local(): lax.ppermute(ring[-1], 'ctx', [(dev, (dev + 1) % 8) for dev in range(8)])]
    all_gather x1 -> x0, blocking collectives: 30.5 us -> none  [local(): fresh = lax.all_gather(columns, 'ctx', axis=0, tiled=True)]
  transfers between devices with their start and end apart: 1 -> 8, of which waited for: 1 -> 8; matrix products, arithmetic and copies ran while one was open for 0% -> 0% of each run, Pallas kernels for 0% -> 0%
where the time goes in v1:
time: 345 us
  blocking collectives  189 us (55%)
  waiting for transfers between devices  104 us (30%)
  matrix products  17.5 us (5%)
  between operations  15 us (4%)
  local copies, waits for them, and re-layouts  9.25 us (3%)
  other arithmetic  8.7 us (3%)
    reduce_scatter x1, waiting for transfers between devices, local(): lax.psum_scatter(jnp.concatenate([grad_k, grad_v], axis=1).astype(jnp.bfl...  59.7 us
    ppermute x7, waiting for transfers between devices, local(): lax.ppermute(ring[-1], 'ctx', [(dev, (dev + 1) % 8) for dev in range(8)])  44.4 us
    all_gather x1, blocking collectives, local(): values = lax.all_gather(document_values, 'ctx', axis=1, tiled=True)[0]  31 us
    all_gather x1, blocking collectives, local(): keys = lax.all_gather(document_keys, 'ctx', axis=1, tiled=True)[0]  30.9 us
    all_gather x1, blocking collectives, local(): lax.all_gather(cart_keys, 'ctx', axis=0, tiled=True)  30.6 us
    all_gather x1, blocking collectives, local(): lax.all_gather(cartridge_values, 'ctx', axis=0, tiled=True)  30.6 us
    psum x1, blocking collectives, local(): squares = lax.psum(jnp.sum(full * full), ('ctx', 'head'))  30.1 us
    all_gather x1, blocking collectives, local(): all_pos = lax.all_gather(doc_pos[0], 'ctx', axis=0, tiled=True)  22.5 us
  transfers between devices with their start and end apart: 8, of which 8 were waited for; matrix products, arithmetic and copies ran while one was open for 0% of the time, Pallas kernels for 0%

profile of v1, /device:TPU:0, one launch (start us, length us, event | category | flops | bytes accessed | tf_op | source)
XLA Modules:
  0.0 344.8 jit_solution(4468315680308180239)
XLA Ops:
  7.2 0.0 reduce-scatter.4.cloned.1.call-start
  7.2 22.5 %all-gather = s32[1,1024]{1,0:T(1,128)S(1)} all-gather(s32[1,128]{1,0:T(1,128)} %param.16), channel_id=2, replica_groups=mesh['dp'=2,'ctx'=8,'head'=2] {'ctx'}, dimensions={1}, use_global_device_ids=true | all-gather | bytes 4608 | tf_op jit(solution)/shard_map/all_gather | solution.py:64
  29.7 30.9 %all_gather.20 = bf16[1,1024,128]{2,1,0:T(8,128)(2,1)S(1)} all-gather(bf16[1,128,128]{2,1,0:T(8,128)(2,1)} %param.14), channel_id=1, replica_groups=mesh['dp'=2,'ctx'=8,'head'=2] {'ctx'}, dimensions={1}, use_global_device_ids=true | all-gather | bytes 294912 | tf_op jit(solution)/shard_map/all_gather | solution.py:79
  60.6 1.3 reshape_squeeze.4
  61.9 31.0 %all_gather.21 = bf16[1,1024,128]{2,1,0:T(8,128)(2,1)S(1)} all-gather(bf16[1,128,128]{2,1,0:T(8,128)(2,1)} %param.15), channel_id=1, replica_groups=mesh['dp'=2,'ctx'=8,'head'=2] {'ctx'}, dimensions={1}, use_global_device_ids=true | all-gather | bytes 294912 | tf_op jit(solution)/shard_map/all_gather | solution.py:80
  92.9 23.1 %while.15 = (s32[]{:T(128)}, f32[2048]{0:T(1024)S(1)}, f32[2048]{0:T(1024)S(1)}, f32[2048,128]{1,0:T(8,128)}, s32[2]{0:T(128)S(1)}, /*index=5*/s32[1024]{0:T(102...) while((s32[]{:T(128)}, f32[2048]{0:T(1024)S(1)}, ...), condition=%wide.region_4.5_spmd.clone, body=%wide.region_1.4_spmd.clone.sunk | while | flops 554444800 | bytes 32434936 | solution.py:93
  92.9 0.8 broadcast_in_dim.101
  93.7 0.1 le.61
  93.8 0.6 dynamic_slice.45
  95.0 0.1 dynamic_slice.46
  95.1 2.7 fusion.75
  97.8 3.5 %fusion.76 = f32[2048]{0:T(1024)S(1)} fusion(f32[512,2048]{1,0:T(8,128)} %get-tuple-element.222, f32[2048]{0:T(1024)S(1)} %select_maximum_fusion.2, s32[2048]{0:T(1024)S(1)} %le.61, s32[512]{0:T(512)S(1)} %dynamic_slice.46), kind=kLoop, calls=%fused_computation.6.clone.1 | loop fusion | flops 6289408 | bytes 4220928 | tf_op jit(solution)/shard_map/while/body/eval_jaxpr/reduce_sum | solution.py:30
  101.3 0.0 copy-done
  101.3 2.5 convolution_add_fusion.4
  103.9 0.7 broadcast_in_dim.101
  104.6 0.1 le.61
  104.7 0.6 dynamic_slice.45
  105.9 0.1 dynamic_slice.46
  106.0 2.7 fusion.75
  108.7 3.5 %fusion.76 = f32[2048]{0:T(1024)S(1)} fusion(f32[512,2048]{1,0:T(8,128)} %get-tuple-element.222, f32[2048]{0:T(1024)S(1)} %select_maximum_fusion.2, s32[2048]{0:T(1024)S(1)} %le.61, s32[512]{0:T(512)S(1)} %dynamic_slice.46), kind=kLoop, calls=%fused_computation.6.clone.1 | loop fusion | flops 6289408 | bytes 4220928 | tf_op jit(solution)/shard_map/while/body/eval_jaxpr/reduce_sum | solution.py:30
  112.2 0.0 copy-done
  112.2 3.7 %convolution_add_fusion.4 = f32[2048,128]{1,0:T(8,128)} fusion(f32[512,2048]{1,0:T(8,128)S(1)} %copy-done, f32[2048]{0:T(1024)S(1)} %select_maximum_fusion.2, s32[2048]{0:T(1024)S(1)} %le.61, s32[512]{0:T(512)S(1)} %dynamic_slice.46, f32[2048,128]{1,0:T(8,128)} %get-tuple-element.242, f32[2048]{0:T(1024)S(1)} %get-tuple-element.224, ...), kind=kOutput, calls=%fused_computation.4.clone.1 | convolution fusion | flops 275513344 | bytes 6449157 | tf_op jit(solution)/shard_map/while/body/eval_jaxpr/dot_general | solution.py:31
  116.0 0.0 copy-done.1
  116.0 0.2 reshape.48
  116.2 0.3 copy.46
  116.5 0.0 copy-done.5
  116.6 30.6 %all_gather.18 = bf16[128,128]{1,0:T(8,128)(2,1)S(1)} all-gather(bf16[16,128]{1,0:T(8,128)(2,1)S(1)} %copy-done.5), channel_id=1, replica_groups=mesh['dp'=2,'ctx'=8,'head'=2] {'ctx'}, dimensions={0}, use_global_device_ids=true | all-gather | bytes 36864 | tf_op jit(solution)/shard_map/all_gather | solution.py:66
  147.2 0.3 fusion.55
  147.5 2.6 copy.45
  150.0 0.0 copy-done.6
  150.0 30.6 %all_gather.22 = bf16[128,128]{1,0:T(8,128)(2,1)S(1)} all-gather(bf16[16,128]{1,0:T(8,128)(2,1)S(1)} %copy-done.6), channel_id=1, replica_groups=mesh['dp'=2,'ctx'=8,'head'=2] {'ctx'}, dimensions={0}, use_global_device_ids=true | all-gather | bytes 36864 | tf_op jit(solution)/shard_map/all_gather | solution.py:67
  180.6 0.2 fusion.34
  180.8 1.8 multiply_reduce_fusion
  182.6 0.0 copy-start.2
  182.6 0.0 copy-start.3
  182.6 0.0 copy-start.4
  182.6 0.4 convolution_convert_fusion
  183.0 0.6 fusion.32
  183.7 0.7 copy.55
  184.4 0.0 reduce-scatter.4.cloned.1.call-update
  184.4 59.7 %reduce-scatter.4.cloned.1.call-done = bf16[16,256]{1,0:T(8,128)(2,1)} async-done(((bf16[128,256]{1,0:T(8,128)(2,1)}), bf16[16,256]{1,0:T(8,128)(2,1)}) %reduce-scatter.4.cloned.1.call-update) | async-done | bytes 8208 | tf_op jit(solution)/shard_map/reduce_scatter | solution.py:120
  244.2 8.7 %psum.14 = f32[16,256]{1,0:T(8,128)S(1)} all-reduce(bf16[16,256]{1,0:T(8,128)(2,1)} %reduce-scatter.4.cloned.1.call-done), channel_id=1, replica_groups=mesh['dp'=2,'ctx'=8,'head'=2] {'dp'}, use_global_device_ids=true, to_apply=%region_8.9 | all-reduce | flops 4096 | bytes 24576 | tf_op jit(solution)/shard_map/psum | solution.py:126
  252.9 0.6 multiply_reduce_fusion.1
  253.5 30.1 %psum.15 = f32[]{:T(128)} all-reduce(f32[]{:T(128)} %multiply_reduce_fusion.1), channel_id=1, replica_groups=mesh['dp'=2,'ctx'=8,'head'=2] {'ctx','head'}, use_global_device_ids=true, to_apply=%region_10.11 | all-reduce | flops 1 | bytes 8 | tf_op jit(solution)/shard_map/psum | solution.py:127
  284.3 0.6 fusion.53
  284.9 4.3 %all-gather.1 = bf16[16,1,256]{2,0,1:T(8,128)(2,1)S(1)} all-gather(bf16[16,1,128]{2,0,1:T(8,128)(2,1)S(1)} %get-tuple-element.138), channel_id=3, replica_groups=mesh['dp'=2,'ctx'=8,'head'=2] {'dp'}, dimensions={2}, use_global_device_ids=true | all-gather | bytes 12288 | tf_op jit(solution)/shard_map/all_gather | solution.py:135
  289.3 0.0 collective-permute-start
  289.3 6.3 %collective-permute-done = bf16[16,256]{1,0:T(8,128)(2,1)S(1)} collective-permute-done((bf16[16,256]{1,0:T(8,128)(2,1)S(1)}, bf16[16,256]{1,0:T(8,128)(2,1)S(1)}, u32[]{:S(2)}, u32[]{:S(2)}) %collective-permute-start) | collective-permute-done | bytes 8224 | tf_op jit(solution)/shard_map/ppermute | solution.py:138
  295.6 0.0 collective-permute-start.1
  295.6 6.3 %collective-permute-done.1 = bf16[16,256]{1,0:T(8,128)(2,1)S(1)} collective-permute-done((bf16[16,256]{1,0:T(8,128)(2,1)S(1)}, bf16[16,256]{1,0:T(8,128)(2,1)S(1)}, u32[]{:S(2)}, u32[]{:S(2)}) %collective-permute-start.1) | collective-permute-done | bytes 8224 | tf_op jit(solution)/shard_map/ppermute | solution.py:138
  302.0 0.0 collective-permute-start.2
  302.0 6.3 %collective-permute-done.2 = bf16[16,256]{1,0:T(8,128)(2,1)S(1)} collective-permute-done((bf16[16,256]{1,0:T(8,128)(2,1)S(1)}, bf16[16,256]{1,0:T(8,128)(2,1)S(1)}, u32[]{:S(2)}, u32[]{:S(2)}) %collective-permute-start.2) | collective-permute-done | bytes 8224 | tf_op jit(solution)/shard_map/ppermute | solution.py:138
  308.3 0.0 collective-permute-start.3
  308.3 6.3 %collective-permute-done.3 = bf16[16,256]{1,0:T(8,128)(2,1)S(1)} collective-permute-done((bf16[16,256]{1,0:T(8,128)(2,1)S(1)}, bf16[16,256]{1,0:T(8,128)(2,1)S(1)}, u32[]{:S(2)}, u32[]{:S(2)}) %collective-permute-start.3) | collective-permute-done | bytes 8224 | tf_op jit(solution)/shard_map/ppermute | solution.py:138
  314.7 0.0 collective-permute-start.4
  314.7 6.3 %collective-permute-done.4 = bf16[16,256]{1,0:T(8,128)(2,1)S(1)} collective-permute-done((bf16[16,256]{1,0:T(8,128)(2,1)S(1)}, bf16[16,256]{1,0:T(8,128)(2,1)S(1)}, u32[]{:S(2)}, u32[]{:S(2)}) %collective-permute-start.4) | collective-permute-done | bytes 8224 | tf_op jit(solution)/shard_map/ppermute | solution.py:138
  321.0 0.0 collective-permute-start.5
  321.0 6.3 %collective-permute-done.5 = bf16[16,256]{1,0:T(8,128)(2,1)S(1)} collective-permute-done((bf16[16,256]{1,0:T(8,128)(2,1)S(1)}, bf16[16,256]{1,0:T(8,128)(2,1)S(1)}, u32[]{:S(2)}, u32[]{:S(2)}) %collective-permute-start.5) | collective-permute-done | bytes 8224 | tf_op jit(solution)/shard_map/ppermute | solution.py:138
  327.4 0.0 collective-permute-start.6
  327.4 6.3 %collective-permute-done.6 = bf16[16,256]{1,0:T(8,128)(2,1)S(1)} collective-permute-done((bf16[16,256]{1,0:T(8,128)(2,1)S(1)}, bf16[16,256]{1,0:T(8,128)(2,1)S(1)}, u32[]{:S(2)}, u32[]{:S(2)}) %collective-permute-start.6) | collective-permute-done | bytes 8224 | tf_op jit(solution)/shard_map/ppermute | solution.py:138
  333.9 0.3 fusion.56
  334.2 0.2 fusion.35
  334.4 2.5 fusion.28
  336.9 1.0 reshape.47
  (39 shorter events, 0.2 us)
Async XLA Ops:
  7.2 237.0 %reduce-scatter.4.cloned.1.call-start = ((), (), s32[]{:S(2)}) async-start(), calls=%async_computation.1 | async-start | bytes 73728 | tf_op jit(solution)/shard_map/reduce_scatter | solution.py:120
  92.9 23.1 %copy-start.1 = (bf16[1,128,2048]{2,1,0:T(8,128)(2,1)S(1)}, bf16[1,128,2048]{2,1,0:T(8,128)(2,1)}, u32[]{:S(2)}) copy-start(bf16[1,128,2048]{2,1,0:T(8,128)(2,1)} %param.13) | copy-start | bytes 1572868
  92.9 23.7 %copy-start.5 = (bf16[16,128]{1,0:T(8,128)(2,1)S(1)}, bf16[16,128]{1,0:T(8,128)(2,1)}, u32[]{:S(2)}) copy-start(bf16[16,128]{1,0:T(8,128)(2,1)} %param.17) | copy-start | bytes 12292
  97.8 3.6 %copy-start = (f32[512,2048]{1,0:T(8,128)S(1)}, f32[512,2048]{1,0:T(8,128)}, u32[]{:S(2)}) copy-start(f32[512,2048]{1,0:T(8,128)} %get-tuple-element.222) | copy-start | bytes 12582916 | tf_op jit(solution)/shard_map/while
  108.7 3.6 %copy-start = (f32[512,2048]{1,0:T(8,128)S(1)}, f32[512,2048]{1,0:T(8,128)}, u32[]{:S(2)}) copy-start(f32[512,2048]{1,0:T(8,128)} %get-tuple-element.222) | copy-start | bytes 12582916 | tf_op jit(solution)/shard_map/while
  116.0 34.1 %copy-start.6 = (bf16[16,128]{1,0:T(8,128)(2,1)S(1)}, bf16[16,128]{1,0:T(8,128)(2,1)}, u32[]{:S(2)}) copy-start(bf16[16,128]{1,0:T(8,128)(2,1)} %param.18) | copy-start | bytes 12292
  182.6 101.7 %copy-start.2 = (f32[16,1,128]{2,1,0:T(1,128)S(1)}, f32[16,1,128]{2,1,0:T(1,128)}, u32[]{:S(2)}) copy-start(f32[16,1,128]{2,1,0:T(1,128)} %param.19) | copy-start | bytes 24580
  182.6 101.7 %copy-start.3 = (f32[16,1,128]{2,1,0:T(1,128)S(1)}, f32[16,1,128]{2,1,0:T(1,128)}, u32[]{:S(2)}) copy-start(f32[16,1,128]{2,1,0:T(1,128)} %param.20) | copy-start | bytes 24580
  182.6 101.7 %copy-start.4 = (f32[16,1,128]{2,1,0:T(1,128)S(1)}, f32[16,1,128]{2,1,0:T(1,128)}, u32[]{:S(2)}) copy-start(f32[16,1,128]{2,1,0:T(1,128)} %param.21) | copy-start | bytes 24580
  289.3 6.3 %collective-permute-start = (bf16[16,256]{1,0:T(8,128)(2,1)S(1)}, bf16[16,256]{1,0:T(8,128)(2,1)S(1)}, u32[]{:S(2)}, u32[]{:S(2)}) collective-permute-start(bf16[16,256]{1,0:T(8,128)(2,1)S(1)} %bitcast.55), channel_id=1, source_target_pairs={{0,2},{2,4},{4,6},{6,8},{8,10},{10,12},{12,14},{14,0},{1,3},{3,5},... | collective-permute-start | bytes 24584 | tf_op jit(solution)/shard_map/ppermute | solution.py:138
  295.6 6.3 %collective-permute-start.1 = (bf16[16,256]{1,0:T(8,128)(2,1)S(1)}, bf16[16,256]{1,0:T(8,128)(2,1)S(1)}, u32[]{:S(2)}, u32[]{:S(2)}) collective-permute-start(bf16[16,256]{1,0:T(8,128)(2,1)S(1)} %collective-permute-done), channel_id=1, source_target_pairs={{0,2},{2,4},{4,6},{6,8},{8,10},{10,12},{12,14},{14,0},{1,3},{3,5},... | collective-permute-start | bytes 24584 | tf_op jit(solution)/shard_map/ppermute | solution.py:138
  302.0 6.3 %collective-permute-start.2 = (bf16[16,256]{1,0:T(8,128)(2,1)S(1)}, bf16[16,256]{1,0:T(8,128)(2,1)S(1)}, u32[]{:S(2)}, u32[]{:S(2)}) collective-permute-start(bf16[16,256]{1,0:T(8,128)(2,1)S(1)} %collective-permute-done.1), channel_id=1, source_target_pairs={{0,2},{2,4},{4,6},{6,8},{8,10},{10,12},{12,14},{14,0},{1,3},{3,5},... | collective-permute-start | bytes 24584 | tf_op jit(solution)/shard_map/ppermute | solution.py:138
  308.3 6.3 %collective-permute-start.3 = (bf16[16,256]{1,0:T(8,128)(2,1)S(1)}, bf16[16,256]{1,0:T(8,128)(2,1)S(1)}, u32[]{:S(2)}, u32[]{:S(2)}) collective-permute-start(bf16[16,256]{1,0:T(8,128)(2,1)S(1)} %collective-permute-done.2), channel_id=1, source_target_pairs={{0,2},{2,4},{4,6},{6,8},{8,10},{10,12},{12,14},{14,0},{1,3},{3,5},... | collective-permute-start | bytes 24584 | tf_op jit(solution)/shard_map/ppermute | solution.py:138
  314.7 6.3 %collective-permute-start.4 = (bf16[16,256]{1,0:T(8,128)(2,1)S(1)}, bf16[16,256]{1,0:T(8,128)(2,1)S(1)}, u32[]{:S(2)}, u32[]{:S(2)}) collective-permute-start(bf16[16,256]{1,0:T(8,128)(2,1)S(1)} %collective-permute-done.3), channel_id=1, source_target_pairs={{0,2},{2,4},{4,6},{6,8},{8,10},{10,12},{12,14},{14,0},{1,3},{3,5},... | collective-permute-start | bytes 24584 | tf_op jit(solution)/shard_map/ppermute | solution.py:138
  321.0 6.3 %collective-permute-start.5 = (bf16[16,256]{1,0:T(8,128)(2,1)S(1)}, bf16[16,256]{1,0:T(8,128)(2,1)S(1)}, u32[]{:S(2)}, u32[]{:S(2)}) collective-permute-start(bf16[16,256]{1,0:T(8,128)(2,1)S(1)} %collective-permute-done.4), channel_id=1, source_target_pairs={{0,2},{2,4},{4,6},{6,8},{8,10},{10,12},{12,14},{14,0},{1,3},{3,5},... | collective-permute-start | bytes 24584 | tf_op jit(solution)/shard_map/ppermute | solution.py:138
  327.4 6.3 %collective-permute-start.6 = (bf16[16,256]{1,0:T(8,128)(2,1)S(1)}, bf16[16,256]{1,0:T(8,128)(2,1)S(1)}, u32[]{:S(2)}, u32[]{:S(2)}) collective-permute-start(bf16[16,256]{1,0:T(8,128)(2,1)S(1)} %collective-permute-done.5), channel_id=1, source_target_pairs={{0,2},{2,4},{4,6},{6,8},{8,10},{10,12},{12,14},{14,0},{1,3},{3,5},... | collective-permute-start | bytes 24584 | tf_op jit(solution)/shard_map/ppermute | solution.py:138
Sparse Core Ops, SparseCore 0:
  184.5 59.5 reduce-scatter.3
